TPU v7x, 32 devices: a whole 2x2x4 slice. The times are simulated.
32 devices in a mesh: parts: 2 (over x), group: 16 (over z, y, core).
Axes of the slice: x: 2, y: 2, z: 4, core: 2. Of those that a mesh axis runs over, the one named last changes fastest.
Arguments:
- solve_cols: bfloat16 [64, 512, 512], P(('parts', 'group')), parts along dimension 0
- region_groups: int32 [32, 4], P('group'), may hold values from 0 to 15, as said below
Outputs:
- schur: float32 [32, 7, 128, 128], P(('parts', 'group')), parts along dimension 0
There are 2 independent parts, one for each index of `parts`. A program takes and returns all parts, laid end to end along the dimension named above; an argument that names none is the same for every part. Nothing has to cross between parts.
Inputs may be any that keep to these rules, and one draw needn't show every extreme that they name: `region_groups`: the 4 groups of a region are 4 consecutive groups modulo 16, in any order. The 2 regions of one device together name 8 consecutive groups modulo 16, each once, so the slots of one device name one group at most 1 times, and exactly 1 times for some group.
All inputs are finite; a program needn't handle non-finite values.
Results may differ from a plain program's by a relative error of at most 0.00048.
Values may be sent and summed in bfloat16 or wider, within the bound.
A program may use at most 128 MiB of HBM per device.

v0:
```python
import functools

import jax
import jax.numpy as jnp
from jax import lax
from jax.experimental import pallas as pl
from jax.experimental.pallas import tpu as pltpu
from jax.sharding import PartitionSpec as P

META = 16
CODE_MAX = 32767.0


def each(count, body, first=0):
    if count - first <= 8:
        for i in range(first, count):
            body(i)
    else:
        lax.fori_loop(first, count, lambda i, _: (body(i), None)[1], None)


def rem(a, b):
    return lax.rem(a, jnp.int32(b))


def classes(slots):
    return [*range(1, (slots + 1) // 2), *([slots // 2] if slots % 2 == 0 else []), 0]


def encode(values, code, scale):
    top = jnp.max(jnp.abs(values), axis=0, keepdims=True)
    shift = jnp.where(top > 1.0, 2.0**-32, 2.0**32)
    inverse = jnp.where(top > 0.0, CODE_MAX / (top * shift), 0.0)
    scaled = (values * shift) * inverse
    rounded = jnp.where(scaled >= 0.0, scaled + 0.5, scaled - 0.5)
    code[...] = rounded.astype(jnp.int32).astype(jnp.int16)
    scale[...] = jnp.broadcast_to(top, scale.shape)


def decode(code, scale):
    return (code[...].astype(jnp.int32).astype(jnp.float32) * (1.0 / CODE_MAX)) * scale[0:1, :]


def kernel(
    total_groups,
    groups,
    cols_hbm,
    out,
    cols,
    gram,
    send,
    recv,
    part,
    code,
    scale,
    code_in,
    scale_in,
    turn,
    turn_scale,
    turn_in,
    turn_scale_in,
    send_sem,
    recv_sem,
    out_sem,
    in_sem,
    turn_sem,
    turn_in_sem,
    cols_sem,
    table,
):
    regions, slots = groups.shape
    width = out.shape[-1]
    units = regions * slots
    reach = slots - 1
    me = lax.axis_index("group")
    home = lax.div(me, units)
    residue = rem(me, units)
    partner = rem(me + units, total_groups)
    order = classes(slots)

    def across(step):
        if units & (units - 1):
            return rem(residue + step, units)
        there, digit = residue, 1
        while digit < units:
            flip = rem(lax.div(jnp.int32(step), jnp.int32(digit)), 2)
            there += digit * flip * (1 - 2 * rem(lax.div(residue, jnp.int32(digit)), 2))
            digit *= 2
        return there

    def peer(step):
        return home * units + across(step)

    def at_offset(k):
        return rem(me + total_groups + k, total_groups)

    def owns_half(group):
        i = rem(group, slots)
        low = i < slots // 2
        return (low & (rem(i, 2) == 0)) | (~low & (rem(i + slots // 2, 2) == 1))

    def if_owner(near, group, body, negate=False):
        if 2 * near == slots:
            owner = owns_half(group)
            pl.when(~owner if negate else owner)(body)
        else:
            body()

    barrier = pltpu.get_barrier_semaphore()

    def greet(step):
        pl.semaphore_signal(barrier, inc=1, device_id={"group": peer(step)})

    each(units, greet, 1)
    pl.semaphore_signal(barrier, inc=1, device_id={"group": partner})

    def fetch(r):
        return pltpu.make_async_copy(cols_hbm.at[r], cols.at[r], cols_sem.at[r])

    each(regions, lambda r: fetch(r).start())

    def plan(step):
        want = across(step)

        def found(unit, best):
            there = groups[lax.div(jnp.int32(unit), jnp.int32(slots)), rem(jnp.int32(unit), slots)]
            return jnp.where(rem(there, units) == want, unit, best)

        unit = jnp.int32(0)
        if units <= 8:
            for u in range(1, units):
                unit = found(u, unit)
        else:
            unit = lax.fori_loop(1, units, found, unit)
        r = lax.div(unit, jnp.int32(slots))
        group = groups[r, rem(unit, slots)]
        others = [groups[r, t] for t in range(slots)]
        place = jnp.int32(-1)
        for o in others:
            place += jnp.where(rem(group - o + total_groups, total_groups) <= reach, 1, 0)
        mark = (lax.div(group, jnp.int32(units)) * slots + place).astype(jnp.float32)
        box = recv if isinstance(step, int) and step == 0 else send
        box[step, 0:META, :] = jnp.full((META, width), mark, jnp.float32).astype(box.dtype)
        for c, near in enumerate(order):
            slot = jnp.int32(0)
            for t in range(1, slots):
                slot = jnp.where(rem(others[t], slots) == rem(want + near, slots), t, slot)
            table[step, c] = unit * slots + slot

    each(units, plan, 1)
    plan(0)

    def gram_of(r):
        fetch(r).wait()
        full = lax.dot_general(
            cols[r], cols[r], (((0,), (0,)), ((), ())), preferred_element_type=jnp.float32
        ).astype(jnp.bfloat16)
        for s in range(slots):
            for t in range(slots):
                gram[(r * slots + s) * slots + t] = full[
                    s * width : (s + 1) * width, t * width : (t + 1) * width
                ]

    each(regions, gram_of)

    def stage(step, c):
        box = recv if isinstance(step, int) and step == 0 else send
        box[step, META + c * width : META + (c + 1) * width, :] = gram[table[step, c]]

    def rows_of(c):
        return pl.ds(0, META + width) if c == 0 else pl.ds(META + c * width, width)

    def unit_copy(step, c):
        return pltpu.make_async_remote_copy(
            src_ref=send.at[step, rows_of(c), :],
            dst_ref=recv.at[step, rows_of(c), :],
            send_sem=send_sem.at[step, c],
            recv_sem=recv_sem.at[step, c],
            device_id={"group": peer(step)},
        )

    def each_unit_copy(c, act):
        def one(step):
            if_owner(order[c], across(step), lambda: act(unit_copy(step, c)))

        if units <= 8:
            for step in sorted(range(1, units), key=lambda e: (e == 1, e.bit_count(), -e)):
                one(step)
        else:
            each(units, one, 1)

    for c in range(len(order)):
        each(units, lambda step: stage(step, c), 1)
        if c == 0:
            pl.semaphore_wait(barrier, units)
        each_unit_copy(c, lambda copy: copy.start())
    for c in range(len(order)):
        stage(0, c)

    def spans_of(c):
        return [0] if order[c] == 0 else [order[c], order[c] - slots]

    def pair(c, boxes, sems, span, device):
        return [
            pltpu.make_async_remote_copy(
                src_ref=src.at[span],
                dst_ref=dst.at[span],
                send_sem=sems[0].at[c, i],
                recv_sem=sems[1].at[c, i],
                device_id={"group": device},
            )
            for i, (src, dst) in enumerate(boxes)
        ]

    def sum_copies(c):
        span = pl.ds(2 * c, len(spans_of(c)))
        boxes = ((code, code_in), (scale, scale_in))
        return pair(c, boxes, (out_sem, in_sem), span, partner)

    def turn_copies(c, j):
        boxes = ((turn, turn_in), (turn_scale, turn_scale_in))
        at = 2 * c + j
        return pair(at, boxes, (turn_sem, turn_in_sem), at, at_offset(spans_of(c)[j]))

    home_mark = (home * slots).astype(jnp.float32)
    away_mark = (rem(home + 1, 2) * slots).astype(jnp.float32)
    tile = min(width, 32)

    def gather_class(c):
        near, spans = order[c], spans_of(c)
        each(units, lambda step: unit_copy(step, c).wait_recv(), 1)

        def add_tile(i):
            at = i * tile

            def add_unit(step, sums):
                mark = jnp.broadcast_to(recv[step, 0:1, :].astype(jnp.float32), (tile, width))
                block = recv[step, pl.ds(META + c * width + at, tile), :].astype(jnp.float32)
                picked = []
                for base in (home_mark, away_mark):
                    ahead = mark - base
                    if near == 0:
                        picked.append((ahead >= 0.0) & (ahead < float(slots)))
                    else:
                        picked.append((ahead >= 0.0) & (ahead < float(slots - near)))
                        picked.append((ahead >= float(slots - near)) & (ahead < float(slots)))
                return tuple(s + jnp.where(p, block, 0.0) for s, p in zip(sums, picked))

            sums = tuple(jnp.zeros((tile, width), jnp.float32) for _ in range(2 * len(spans)))
            if units <= 8:
                for step in range(units):
                    sums = add_unit(step, sums)
            else:
                sums = lax.fori_loop(0, units, add_unit, sums)
            for j, span in enumerate(spans):
                out[span + reach, pl.ds(at, tile), :] = sums[j]
                part[2 * c + j, pl.ds(at, tile), :] = sums[len(spans) + j]

        each(width // tile, add_tile)
        for j in range(len(spans)):
            encode(part[2 * c + j], code.at[2 * c + j], scale.at[2 * c + j])
        for copy in sum_copies(c):
            copy.start()

    def finish_class(c):
        for copy in sum_copies(c):
            copy.wait_recv()
        for j, span in enumerate(spans_of(c)):
            at = 2 * c + j
            total = out[span + reach] + decode(code_in.at[at], scale_in.at[at])
            out[span + reach] = total
            if span:
                encode(total.T, turn.at[at], turn_scale.at[at])
                for copy in turn_copies(c, j):
                    copy.start()

    def place_turned(c):
        for j, span in enumerate(spans_of(c)):
            for copy in turn_copies(c, j):
                copy.wait_recv()
            out[reach - span] = decode(turn_in.at[2 * c + j], turn_scale_in.at[2 * c + j])

    def drain(c):
        for copy in sum_copies(c):
            copy.wait_send()
        if order[c]:
            for j in range(2):
                for copy in turn_copies(c, j):
                    copy.wait_send()

    last = len(order) - 1
    for c in range(last + 1):
        if_owner(order[c], me, functools.partial(gather_class, c))
        if c:
            if_owner(order[c - 1], me, functools.partial(finish_class, c - 1))
    for c in range(last):
        if_owner(order[c], me, functools.partial(place_turned, c), negate=True)
    finish_class(last)

    for c in range(last + 1):
        each_unit_copy(c, lambda copy: copy.wait_send())
        if_owner(order[c], me, functools.partial(drain, c))


def shards(solve_cols, region_groups):
    regions, slots = region_groups.shape
    width = solve_cols.shape[2] // slots
    total_groups = lax.axis_size("group")
    units = regions * slots
    assert total_groups == 2 * units
    spans = 2 * slots - 1
    count = len(classes(slots))
    sent = 2 * count - 1
    box = pltpu.VMEM((units, META + count * width, width), jnp.bfloat16)
    coded = [pltpu.VMEM((sent, width, width), jnp.int16), pltpu.VMEM((sent, 8, width), jnp.float32)]
    vmem = pl.BlockSpec(memory_space=pltpu.VMEM)
    sums = pl.pallas_call(
        functools.partial(kernel, total_groups),
        out_shape=pltpu.VMEM((spans, width, width), jnp.float32),
        in_specs=[pl.BlockSpec(memory_space=pltpu.SMEM), pl.BlockSpec(memory_space=pl.ANY)],
        out_specs=vmem,
        scratch_shapes=[
            pltpu.VMEM(solve_cols.shape, solve_cols.dtype),
            pltpu.VMEM((units * slots, width, width), jnp.bfloat16),
            box,
            box,
            pltpu.VMEM((sent, width, width), jnp.float32),
            *(coded * 4),
            pltpu.SemaphoreType.DMA((units, count)),
            pltpu.SemaphoreType.DMA((units, count)),
            pltpu.SemaphoreType.DMA((count, 2)),
            pltpu.SemaphoreType.DMA((count, 2)),
            pltpu.SemaphoreType.DMA((sent, 2)),
            pltpu.SemaphoreType.DMA((sent, 2)),
            pltpu.SemaphoreType.DMA((regions,)),
            pltpu.SMEM((units, count), jnp.int32),
        ],
        compiler_params=pltpu.CompilerParams(
            collective_id=0, has_side_effects=True, vmem_limit_bytes=60 * 1024 * 1024
        ),
    )(region_groups, solve_cols)
    return sums[None]


def solution(mesh):
    return jax.shard_map(
        shards,
        mesh=mesh,
        in_specs=(P(("parts", "group"), None, None), P("group", None)),
        out_specs=P(("parts", "group"), None, None, None),
        check_vma=False,
    )
```

profile of v0, /device:TPU:0, one launch (start us, length us, event | category | flops | bytes accessed | tf_op | source)
XLA Modules:
  0.0 22.8 jit_solution(1573559887100023572)
XLA Ops:
  0.0 22.0 %shard_map.28 = f32[7,128,128]{2,1,0:T(8,128)S(1)} custom-call(s32[2,4]{1,0:T(2,128)} %groups.1, bf16[2,512,512]{2,1,0:T(8,128)(2,1)} %cols_hbm.1), custom_call_target="tpu_custom_call" | custom-call | tf_op jit(solution)/shard_map/pallas_call | solution.py:317
  22.0 0.8 %copy.4 = f32[1,7,128,128]{3,2,1,0:T(8,128)} copy(f32[1,7,128,128]{3,2,1,0:T(8,128)S(1)} %bitcast.1) | data formatting | bytes 917504
where the time goes:
time: 23.1 us; the launch traced here: 22.8 us
  Pallas kernels  22 us (95%)
  local copies, waits for them, and re-layouts  0.77 us (3%)
    pallas_call x1, Pallas kernels, shards(): pl.pallas_call(functools.partial(kernel, total_groups), out_shape=pltpu.V...  22 us
    unnamed x1, local copies, waits for them, and re-layouts  0.77 us

commit v1 on v0

--- a/solution.py
+++ b/solution.py
@@ -43,7 +43,7 @@
 
 def kernel(
     total_groups,
-    groups,
+    groups_hbm,
     cols_hbm,
     out,
     cols,
@@ -67,7 +67,11 @@
     turn_in_sem,
     cols_sem,
     table,
+    groups,
+    groups_sem,
 ):
+    groups_copy = pltpu.make_async_copy(groups_hbm, groups, groups_sem)
+    groups_copy.start()
     regions, slots = groups.shape
     width = out.shape[-1]
     units = regions * slots
@@ -147,6 +151,7 @@
                 slot = jnp.where(rem(others[t], slots) == rem(want + near, slots), t, slot)
             table[step, c] = unit * slots + slot
 
+    groups_copy.wait()
     each(units, plan, 1)
     plan(0)
 
@@ -317,7 +322,7 @@
     sums = pl.pallas_call(
         functools.partial(kernel, total_groups),
         out_shape=pltpu.VMEM((spans, width, width), jnp.float32),
-        in_specs=[pl.BlockSpec(memory_space=pltpu.SMEM), pl.BlockSpec(memory_space=pl.ANY)],
+        in_specs=[pl.BlockSpec(memory_space=pl.ANY), pl.BlockSpec(memory_space=pl.ANY)],
         out_specs=vmem,
         scratch_shapes=[
             pltpu.VMEM(solve_cols.shape, solve_cols.dtype),
@@ -334,6 +339,8 @@
             pltpu.SemaphoreType.DMA((sent, 2)),
             pltpu.SemaphoreType.DMA((regions,)),
             pltpu.SMEM((units, count), jnp.int32),
+            pltpu.SMEM(region_groups.shape, jnp.int32),
+            pltpu.SemaphoreType.DMA(()),
         ],
         compiler_params=pltpu.CompilerParams(
             collective_id=0, has_side_effects=True, vmem_limit_bytes=60 * 1024 * 1024

time: 23.1 us -> 22.3 us (0.965)
  Pallas kernels: 22 us -> 21.3 us
    pallas_call x1, Pallas kernels: 22 us -> 21.3 us  [shards(): pl.pallas_call(functools.partial(kernel, total_groups), out_shape=pltpu.V...]
where the time goes in v1:
time: 22.3 us; the launch traced here: 22.1 us
  Pallas kernels  21.3 us (96%)
  local copies, waits for them, and re-layouts  0.77 us (3%)
    pallas_call x1, Pallas kernels, shards(): pl.pallas_call(functools.partial(kernel, total_groups), out_shape=pltpu.V...  21.3 us
    unnamed x1, local copies, waits for them, and re-layouts  0.77 us

profile of v1, /device:TPU:0, one launch (start us, length us, event | category | flops | bytes accessed | tf_op | source)
XLA Modules:
  0.0 22.1 jit_solution(6265004621148150986)
XLA Ops:
  0.0 21.3 %shard_map.28 = f32[7,128,128]{2,1,0:T(8,128)S(1)} custom-call(s32[2,4]{1,0:T(2,128)} %groups_hbm.1, bf16[2,512,512]{2,1,0:T(8,128)(2,1)} %cols_hbm.1), custom_call_target="tpu_custom_call" | custom-call | tf_op jit(solution)/shard_map/pallas_call | solution.py:322
  21.3 0.8 %copy.4 = f32[1,7,128,128]{3,2,1,0:T(8,128)} copy(f32[1,7,128,128]{3,2,1,0:T(8,128)S(1)} %bitcast.1) | data formatting | bytes 917504

commit v2 on v1

--- a/solution.py
+++ b/solution.py
@@ -9,6 +9,7 @@
 
 META = 16
 CODE_MAX = 32767.0
+CUTS = {}
 
 
 def each(count, body, first=0):
@@ -39,6 +40,52 @@
 
 def decode(code, scale):
     return (code[...].astype(jnp.int32).astype(jnp.float32) * (1.0 / CODE_MAX)) * scale[0:1, :]
+
+
+def pieces_of(slots, width, cuts):
+    pieces, start = [], META
+    for c, near in enumerate(classes(slots)):
+        count = cuts.get(near, 1)
+        rows = width // count if near else width // 2
+        for i in range(count):
+            pieces.append((c, near, i * rows, rows, start))
+            start += rows
+    return pieces, start
+
+
+def lanes_rows(rows, width):
+    shape = (rows, width)
+    return lax.broadcasted_iota(jnp.int32, shape, 1), lax.broadcasted_iota(jnp.int32, shape, 0)
+
+
+def fold(square):
+    width = square.shape[1]
+    half = width // 2
+    lane, row = lanes_rows(half, width)
+    low = pltpu.roll(square[half:], half, 1)
+    folded = jnp.where((lane >= half) | (lane <= row), square[:half], low)
+    diagonal = jnp.sum(jnp.where(lane == row, low, 0.0), axis=0, keepdims=True)
+    return folded, diagonal
+
+
+def unfold(folded, diagonal):
+    half, width = folded.shape
+    lane, row = lanes_rows(half, width)
+    turned = jnp.concatenate([folded, jnp.zeros_like(folded)], axis=0).T
+    top = jnp.where((lane >= half) | (lane <= row), folded, turned[:half])
+    corner = jnp.where(lane > row, folded, jnp.where(lane < row, turned[:half], diagonal))
+    return top, jnp.where(lane < half, turned[half:], pltpu.roll(corner, half, 1))
+
+
+def steps_of(pieces):
+    last = len(pieces) - 1
+    steps = [("send", p) for p in range(last)]
+    steps += [("own", p) for p in range(last + 1)]
+    steps += [("gather", 0), ("send", last)]
+    steps += [("gather", p) for p in range(1, last)]
+    steps += [("finish", 0), ("gather", last)]
+    steps += [("finish", p) for p in range(1, last + 1)]
+    return steps + [("place", near) for near in dict.fromkeys(q[1] for q in pieces) if near]
 
 
 def kernel(
@@ -51,6 +98,7 @@
     send,
     recv,
     part,
+    folded_sum,
     code,
     scale,
     code_in,
@@ -81,6 +129,8 @@
     residue = rem(me, units)
     partner = rem(me + units, total_groups)
     order = classes(slots)
+    half = width // 2
+    pieces, _ = pieces_of(slots, width, CUTS)
 
     def across(step):
         if units & (units - 1):
@@ -159,34 +209,46 @@
         fetch(r).wait()
         full = lax.dot_general(
             cols[r], cols[r], (((0,), (0,)), ((), ())), preferred_element_type=jnp.float32
-        ).astype(jnp.bfloat16)
+        )
         for s in range(slots):
             for t in range(slots):
-                gram[(r * slots + s) * slots + t] = full[
-                    s * width : (s + 1) * width, t * width : (t + 1) * width
-                ]
+                block = full[s * width : (s + 1) * width, t * width : (t + 1) * width]
+                at = (r * slots + s) * slots + t
+                if s != t:
+                    gram[at] = block.astype(jnp.bfloat16)
+                else:
+                    folded, diagonal = fold(block)
+                    gram[at, :half, :] = folded.astype(jnp.bfloat16)
+                    gram[at, half : half + META, :] = jnp.broadcast_to(
+                        diagonal, (META, width)
+                    ).astype(jnp.bfloat16)
 
     each(regions, gram_of)
 
-    def stage(step, c):
+    def stage(step, p):
+        c, near, at, rows, start = pieces[p]
         box = recv if isinstance(step, int) and step == 0 else send
-        box[step, META + c * width : META + (c + 1) * width, :] = gram[table[step, c]]
-
-    def rows_of(c):
-        return pl.ds(0, META + width) if c == 0 else pl.ds(META + c * width, width)
-
-    def unit_copy(step, c):
+        box[step, start : start + rows, :] = gram[table[step, c], at : at + rows, :]
+        if p == 0:
+            diagonal = gram[table[step, len(order) - 1], half : half + META, :].astype(jnp.float32)
+            mark = box[step, 0:META, :].astype(jnp.float32)
+            _, row = lanes_rows(META, width)
+            box[step, 0:META, :] = jnp.where(row < 8, mark, diagonal).astype(box.dtype)
+
+    def unit_copy(step, p):
+        c, near, at, rows, start = pieces[p]
+        span = pl.ds(0, META + rows) if p == 0 else pl.ds(start, rows)
         return pltpu.make_async_remote_copy(
-            src_ref=send.at[step, rows_of(c), :],
-            dst_ref=recv.at[step, rows_of(c), :],
-            send_sem=send_sem.at[step, c],
-            recv_sem=recv_sem.at[step, c],
+            src_ref=send.at[step, span, :],
+            dst_ref=recv.at[step, span, :],
+            send_sem=send_sem.at[step, p],
+            recv_sem=recv_sem.at[step, p],
             device_id={"group": peer(step)},
         )
 
-    def each_unit_copy(c, act):
+    def each_unit_copy(p, act):
         def one(step):
-            if_owner(order[c], across(step), lambda: act(unit_copy(step, c)))
+            if_owner(pieces[p][1], across(step), lambda: act(unit_copy(step, p)))
 
         if units <= 8:
             for step in sorted(range(1, units), key=lambda e: (e == 1, e.bit_count(), -e)):
@@ -194,53 +256,76 @@
         else:
             each(units, one, 1)
 
-    for c in range(len(order)):
-        each(units, lambda step: stage(step, c), 1)
-        if c == 0:
-            pl.semaphore_wait(barrier, units)
-        each_unit_copy(c, lambda copy: copy.start())
-    for c in range(len(order)):
-        stage(0, c)
-
-    def spans_of(c):
-        return [0] if order[c] == 0 else [order[c], order[c] - slots]
-
-    def pair(c, boxes, sems, span, device):
+    def send_piece(p):
+        each_unit_copy(p, lambda copy: copy.start())
+
+    def spans_of(near):
+        return [0] if near == 0 else [near, near - slots]
+
+    def pair(at, boxes, sems, device):
         return [
             pltpu.make_async_remote_copy(
-                src_ref=src.at[span],
-                dst_ref=dst.at[span],
-                send_sem=sems[0].at[c, i],
-                recv_sem=sems[1].at[c, i],
+                src_ref=src,
+                dst_ref=dst,
+                send_sem=sems[0].at[at, i],
+                recv_sem=sems[1].at[at, i],
                 device_id={"group": device},
             )
             for i, (src, dst) in enumerate(boxes)
         ]
 
-    def sum_copies(c):
-        span = pl.ds(2 * c, len(spans_of(c)))
-        boxes = ((code, code_in), (scale, scale_in))
-        return pair(c, boxes, (out_sem, in_sem), span, partner)
-
-    def turn_copies(c, j):
-        boxes = ((turn, turn_in), (turn_scale, turn_scale_in))
-        at = 2 * c + j
-        return pair(at, boxes, (turn_sem, turn_in_sem), at, at_offset(spans_of(c)[j]))
+    def sum_copies(p):
+        c, near, at, rows, _ = pieces[p]
+        spans = len(spans_of(near))
+        values = pl.ds(2 * c, spans), pl.ds(at, rows if near else half)
+        tops = pl.ds(2 * p, 2)
+        boxes = ((code.at[*values], code_in.at[*values]), (scale.at[tops], scale_in.at[tops]))
+        return pair(p, boxes, (out_sem, in_sem), partner)
+
+    def turn_copies(p, j):
+        c, near, at, rows, _ = pieces[p]
+        values = 2 * c + j, pl.ds(at, rows)
+        boxes = (
+            (turn.at[*values], turn_in.at[*values]),
+            (turn_scale.at[2 * p + j], turn_scale_in.at[2 * p + j]),
+        )
+        return pair(2 * p + j, boxes, (turn_sem, turn_in_sem), at_offset(spans_of(near)[j]))
 
     home_mark = (home * slots).astype(jnp.float32)
     away_mark = (rem(home + 1, 2) * slots).astype(jnp.float32)
-    tile = min(width, 32)
-
-    def gather_class(c):
-        near, spans = order[c], spans_of(c)
-        each(units, lambda step: unit_copy(step, c).wait_recv(), 1)
+
+    def add_diagonal(p):
+        c = pieces[p][0]
+
+        def add_unit(step, sums):
+            ahead = recv[step, 0:1, :].astype(jnp.float32)
+            row = recv[step, 8:9, :].astype(jnp.float32)
+            picked = []
+            for base in (home_mark, away_mark):
+                picked.append((ahead >= base) & (ahead < base + float(slots)))
+            return tuple(s + jnp.where(q, row, 0.0) for s, q in zip(sums, picked))
+
+        sums = tuple(jnp.zeros((1, width), jnp.float32) for _ in range(2))
+        if units <= 8:
+            for step in range(units):
+                sums = add_unit(step, sums)
+        else:
+            sums = lax.fori_loop(0, units, add_unit, sums)
+        folded_sum[half : half + 8, :] = jnp.broadcast_to(sums[0], (8, width))
+        scale[2 * p + 1] = sums[1]
+
+    def gather(p):
+        c, near, at, rows, start = pieces[p]
+        spans = spans_of(near)
+        tile = META if rows % 32 else 32
+        each(units, lambda step: unit_copy(step, p).wait_recv(), 1)
 
         def add_tile(i):
-            at = i * tile
+            row = i * tile
 
             def add_unit(step, sums):
                 mark = jnp.broadcast_to(recv[step, 0:1, :].astype(jnp.float32), (tile, width))
-                block = recv[step, pl.ds(META + c * width + at, tile), :].astype(jnp.float32)
+                block = recv[step, pl.ds(start + row, tile), :].astype(jnp.float32)
                 picked = []
                 for base in (home_mark, away_mark):
                     ahead = mark - base
@@ -249,7 +334,7 @@
                     else:
                         picked.append((ahead >= 0.0) & (ahead < float(slots - near)))
                         picked.append((ahead >= float(slots - near)) & (ahead < float(slots)))
-                return tuple(s + jnp.where(p, block, 0.0) for s, p in zip(sums, picked))
+                return tuple(s + jnp.where(q, block, 0.0) for s, q in zip(sums, picked))
 
             sums = tuple(jnp.zeros((tile, width), jnp.float32) for _ in range(2 * len(spans)))
             if units <= 8:
@@ -258,53 +343,85 @@
             else:
                 sums = lax.fori_loop(0, units, add_unit, sums)
             for j, span in enumerate(spans):
-                out[span + reach, pl.ds(at, tile), :] = sums[j]
-                part[2 * c + j, pl.ds(at, tile), :] = sums[len(spans) + j]
-
-        each(width // tile, add_tile)
+                if near:
+                    out[span + reach, pl.ds(at + row, tile), :] = sums[j]
+                else:
+                    folded_sum[pl.ds(row, tile), :] = sums[j]
+                part[2 * c + j, pl.ds(at + row, tile), :] = sums[len(spans) + j]
+
+        each(rows // tile, add_tile)
+        if not near:
+            add_diagonal(p)
         for j in range(len(spans)):
-            encode(part[2 * c + j], code.at[2 * c + j], scale.at[2 * c + j])
-        for copy in sum_copies(c):
+            if near:
+                values = pl.ds(at, rows)
+                encode(part[2 * c + j, values, :], code.at[2 * c + j, values], scale.at[2 * p + j])
+            else:
+                encode(part[2 * c, :half, :], code.at[2 * c, :half], scale.at[2 * p])
+        for copy in sum_copies(p):
             copy.start()
 
-    def finish_class(c):
-        for copy in sum_copies(c):
+    def finish(p):
+        c, near, at, rows, _ = pieces[p]
+        for copy in sum_copies(p):
             copy.wait_recv()
-        for j, span in enumerate(spans_of(c)):
-            at = 2 * c + j
-            total = out[span + reach] + decode(code_in.at[at], scale_in.at[at])
-            out[span + reach] = total
-            if span:
-                encode(total.T, turn.at[at], turn_scale.at[at])
-                for copy in turn_copies(c, j):
-                    copy.start()
-
-    def place_turned(c):
-        for j, span in enumerate(spans_of(c)):
-            for copy in turn_copies(c, j):
-                copy.wait_recv()
-            out[reach - span] = decode(turn_in.at[2 * c + j], turn_scale_in.at[2 * c + j])
-
-    def drain(c):
-        for copy in sum_copies(c):
+        if not near:
+            total = folded_sum[:half, :] + decode(code_in.at[2 * c, :half], scale_in.at[2 * p])
+            diagonal = folded_sum[half : half + 1, :] + scale_in[2 * p + 1]
+            out[reach, :half, :], out[reach, half:, :] = unfold(total, diagonal)
+            return
+        for j, span in enumerate(spans_of(near)):
+            values = pl.ds(at, rows)
+            total = out[span + reach, values, :] + decode(
+                code_in.at[2 * c + j, values], scale_in.at[2 * p + j]
+            )
+            out[span + reach, values, :] = total
+            encode(total, turn.at[2 * c + j, values], turn_scale.at[2 * p + j])
+            for copy in turn_copies(p, j):
+                copy.start()
+
+    def place(near):
+        for j, span in enumerate(spans_of(near)):
+            rows_in = []
+            for p, (c, its_near, at, rows, _) in enumerate(pieces):
+                if its_near == near:
+                    for copy in turn_copies(p, j):
+                        copy.wait_recv()
+                    rows_in.append(
+                        decode(turn_in.at[2 * c + j, pl.ds(at, rows)], turn_scale_in.at[2 * p + j])
+                    )
+            block = rows_in[0] if len(rows_in) == 1 else jnp.concatenate(rows_in, axis=0)
+            out[reach - span] = block.T
+
+    def drain(p):
+        for copy in sum_copies(p):
             copy.wait_send()
-        if order[c]:
+        if pieces[p][1]:
             for j in range(2):
-                for copy in turn_copies(c, j):
+                for copy in turn_copies(p, j):
                     copy.wait_send()
 
-    last = len(order) - 1
-    for c in range(last + 1):
-        if_owner(order[c], me, functools.partial(gather_class, c))
-        if c:
-            if_owner(order[c - 1], me, functools.partial(finish_class, c - 1))
-    for c in range(last):
-        if_owner(order[c], me, functools.partial(place_turned, c), negate=True)
-    finish_class(last)
-
-    for c in range(last + 1):
-        each_unit_copy(c, lambda copy: copy.wait_send())
-        if_owner(order[c], me, functools.partial(drain, c))
+    def owned(act, p):
+        if_owner(pieces[p][1], me, functools.partial(act, p))
+
+    for act, p in steps_of(pieces):
+        if act == "send":
+            each(units, lambda step: stage(step, p), 1)
+            if p == 0:
+                pl.semaphore_wait(barrier, units)
+            send_piece(p)
+        elif act == "own":
+            stage(0, p)
+        elif act == "gather":
+            owned(gather, p)
+        elif act == "finish":
+            owned(finish, p)
+        else:
+            if_owner(p, me, functools.partial(place, p), negate=True)
+
+    for p in range(len(pieces)):
+        each_unit_copy(p, lambda copy: copy.wait_send())
+        owned(drain, p)
 
 
 def shards(solve_cols, region_groups):
@@ -316,8 +433,10 @@
     spans = 2 * slots - 1
     count = len(classes(slots))
     sent = 2 * count - 1
-    box = pltpu.VMEM((units, META + count * width, width), jnp.bfloat16)
-    coded = [pltpu.VMEM((sent, width, width), jnp.int16), pltpu.VMEM((sent, 8, width), jnp.float32)]
+    pieces, height = pieces_of(slots, width, CUTS)
+    many = len(pieces)
+    box = pltpu.VMEM((units, height, width), jnp.bfloat16)
+    coded = [pltpu.VMEM((sent, width, width), jnp.int16), pltpu.VMEM((2 * many, 1, width), jnp.float32)]
     vmem = pl.BlockSpec(memory_space=pltpu.VMEM)
     sums = pl.pallas_call(
         functools.partial(kernel, total_groups),
@@ -330,13 +449,11 @@
             box,
             box,
             pltpu.VMEM((sent, width, width), jnp.float32),
+            pltpu.VMEM((width // 2 + 8, width), jnp.float32),
             *(coded * 4),
-            pltpu.SemaphoreType.DMA((units, count)),
-            pltpu.SemaphoreType.DMA((units, count)),
-            pltpu.SemaphoreType.DMA((count, 2)),
-            pltpu.SemaphoreType.DMA((count, 2)),
-            pltpu.SemaphoreType.DMA((sent, 2)),
-            pltpu.SemaphoreType.DMA((sent, 2)),
+            *([pltpu.SemaphoreType.DMA((units, many))] * 2),
+            *([pltpu.SemaphoreType.DMA((many, 2))] * 2),
+            *([pltpu.SemaphoreType.DMA((2 * many, 2))] * 2),
             pltpu.SemaphoreType.DMA((regions,)),
             pltpu.SMEM((units, count), jnp.int32),
             pltpu.SMEM(region_groups.shape, jnp.int32),

time: 22.3 us -> 21.9 us (0.982)
  Pallas kernels: 21.3 us -> 21 us
    pallas_call x1, Pallas kernels: 21.3 us -> 21 us  [shards(): pl.pallas_call(functools.partial(kernel, total_groups), out_shape=pltpu.V...]
where the time goes in v2:
time: 21.9 us; the launch traced here: 21.7 us
  Pallas kernels  21 us (96%)
  local copies, waits for them, and re-layouts  0.77 us (4%)
    pallas_call x1, Pallas kernels, shards(): pl.pallas_call(functools.partial(kernel, total_groups), out_shape=pltpu.V...  21 us
    unnamed x1, local copies, waits for them, and re-layouts  0.77 us

profile of v2, /device:TPU:0, one launch (start us, length us, event | category | flops | bytes accessed | tf_op | source)
XLA Modules:
  0.0 21.7 jit_solution(8854698833048585514)
XLA Ops:
  0.0 21.0 %shard_map.28 = f32[7,128,128]{2,1,0:T(8,128)S(1)} custom-call(s32[2,4]{1,0:T(2,128)} %groups_hbm.1, bf16[2,512,512]{2,1,0:T(8,128)(2,1)} %cols_hbm.1), custom_call_target="tpu_custom_call" | custom-call | tf_op jit(solution)/shard_map/pallas_call | solution.py:441
  21.0 0.8 %copy.4 = f32[1,7,128,128]{3,2,1,0:T(8,128)} copy(f32[1,7,128,128]{3,2,1,0:T(8,128)S(1)} %bitcast.1) | data formatting | bytes 917504
